TPU v7x, 256 devices: a whole 4x4x8 slice. The times are simulated.
256 devices in a mesh: rows: 32 (over y, z), tensor: 8 (over x, core).
Axes of the slice: x: 4, y: 4, z: 8, core: 2. Of those that a mesh axis runs over, the one named last changes fastest.
Arguments:
- token_ids: int32 [256, 4], replicated, may hold values from 0 to 65535
- cache_lengths: int32 [256], P('rows'), may hold values from 160 to 1280, as said below
- doc_ids: int32 [256], replicated, may hold values from 0 to 31
- embed_table: bfloat16 [65536, 8192], P('tensor', 'rows'), may hold values from -10.5 to 10.5
- cache_keys: bfloat16 [256, 1280, 1024], P('rows', None, 'tensor'), may hold values from -700 to 700
- cache_values: bfloat16 [256, 1280, 1024], P('rows', None, 'tensor'), may hold values from -6 to 6
- decode_gain: float32 [8192], P('rows'), may hold values from 0.1 to 1.9
- decode_query: bfloat16 [8192, 8192], P('rows', 'tensor'), may hold values from -0.0625 to 0.0625
- decode_key: bfloat16 [8192, 1024], P('rows', 'tensor'), may hold values from -0.0625 to 0.0625
- decode_value: bfloat16 [8192, 1024], P('rows', 'tensor'), may hold values from -0.0625 to 0.0625
- decode_out: bfloat16 [8192, 8192], P('tensor', 'rows'), may hold values from -0.0625 to 0.0625
- reduce_gain: float32 [8192], P('rows'), may hold values from 0.8 to 10
- reduce_query: bfloat16 [8192, 8192], P('rows', 'tensor'), may hold values from -0.0625 to 0.0625
- reduce_key: bfloat16 [8192, 1024], P('rows', 'tensor'), may hold values from -0.0625 to 0.0625
- reduce_value: bfloat16 [8192, 1024], P('rows', 'tensor'), may hold values from -0.0625 to 0.0625
- reduce_out: bfloat16 [8192, 8192], P('tensor', 'rows'), may hold values from -0.0625 to 0.0625
Outputs:
- reduced: bfloat16 [1024, 8192], P(None, 'rows')
Inputs may be any that keep to these rules, and one draw needn't show every extreme that they name: Passage row c holds cache entries at positions below cache_lengths[c]; one row in every draw has a full cache of 1280.
All inputs are finite; a program needn't handle non-finite values.
Results may differ from a plain program's by a relative error of at most 0.035.
The roundings to bfloat16 on the way count: a program that leaves them out, or rounds other values in their place, can miss the bound.
Values may be sent and summed in bfloat16 or wider, within the bound.
A program may use at most 64 MiB of HBM per device.

v0:
```python
import jax
import jax.numpy as jnp
from jax import lax
from jax.sharding import PartitionSpec as P

D = 8192
HEAD_DIM = 128
EPSILON = 1e-05
ROPE_BASE = 500000.0


def rotate(vectors, positions):
    half_dim = vectors.shape[-1] // 2
    frequencies = ROPE_BASE ** (-2.0 * jnp.arange(half_dim, dtype=jnp.float32) / vectors.shape[-1])
    angles = positions.astype(jnp.float32)[..., None] * frequencies
    cosine = jnp.cos(angles)
    sine_part = jnp.sin(angles)
    lower_half = vectors[..., :half_dim]
    upper_half = vectors[..., half_dim:]
    return jnp.concatenate(
        [
            lower_half * cosine - upper_half * sine_part,
            upper_half * cosine + lower_half * sine_part,
        ],
        axis=-1,
    )


def width_total(partial_value):
    return lax.psum(partial_value, "tensor")


def row_scale(summed):
    return lax.rsqrt(summed / D + EPSILON)


def head_terms(normed, matrices, squares, groups):
    partial = jnp.concatenate(
        [jnp.dot(normed, matrix, preferred_element_type=jnp.float32) for matrix in matrices], axis=1
    )
    tokens, cols = partial.shape
    own = tokens // groups
    payload = jnp.concatenate(
        [partial.reshape(groups, own * cols), squares.reshape(groups, own)], axis=1
    ).reshape(groups, 8, (own * cols + own) // 8)
    summed = lax.psum_scatter(payload, "rows", scatter_dimension=0, tiled=True)
    summed = summed.reshape(own * cols + own)
    return (summed[: own * cols].reshape(own, cols), summed[own * cols :])


def head_mix(attended, matrix):
    return jnp.dot(
        lax.all_gather(attended, "rows", axis=0, tiled=True),
        matrix,
        preferred_element_type=jnp.float32,
    )


def per_device(
    token_ids,
    cache_lengths,
    doc_ids,
    embed_table,
    cache_keys,
    cache_values,
    decode_gain,
    decode_query,
    decode_key,
    decode_value,
    decode_out,
    reduce_gain,
    reduce_query,
    reduce_key,
    reduce_value,
    reduce_out,
):
    step_count = token_ids.shape[1]
    passage_count = token_ids.shape[0]
    token_count = passage_count * step_count
    own_passages = cache_lengths.shape[0]
    own_tokens = own_passages * step_count
    row_first = lax.axis_index("rows") * own_tokens
    query_cols = decode_query.shape[1]
    kv_cols = decode_key.shape[1]
    local_heads = query_cols // HEAD_DIM
    local_kv = kv_cols // HEAD_DIM
    group_size = local_heads // local_kv
    score_scale = HEAD_DIM ** (-0.5)
    step_ids = jnp.arange(step_count, dtype=jnp.int32)
    vocab_part = embed_table.shape[0]
    local_ids = token_ids.reshape(token_count) - lax.axis_index("tensor") * vocab_part
    inside = (local_ids >= 0) & (local_ids < vocab_part)
    picked = jnp.take(embed_table, jnp.clip(local_ids, 0, vocab_part - 1), axis=0)
    picked = jnp.where(inside[:, None], picked, jnp.zeros_like(picked))
    embedded = width_total(picked).astype(jnp.float32)
    row_groups = token_count // own_tokens
    normed = (embedded * decode_gain[None, :]).astype(jnp.bfloat16)
    projected, dec_squares = head_terms(
        normed,
        (decode_query, decode_key, decode_value),
        jnp.sum(embedded * embedded, axis=1),
        row_groups,
    )
    projected = projected * row_scale(dec_squares)[:, None]
    positions = (cache_lengths[:, None] + step_ids[None, :]).reshape(own_tokens, 1)
    queries = rotate(
        projected[:, :query_cols].reshape(own_tokens, local_heads, HEAD_DIM), positions
    ).astype(jnp.bfloat16)
    keys_new = rotate(
        projected[:, query_cols : query_cols + kv_cols].reshape(own_tokens, local_kv, HEAD_DIM),
        positions,
    ).astype(jnp.bfloat16)
    values_new = projected[:, query_cols + kv_cols :].astype(jnp.bfloat16)
    queries = queries.reshape(own_passages, step_count, local_kv, group_size, HEAD_DIM)
    keys_new = keys_new.reshape(own_passages, step_count, local_kv, HEAD_DIM)
    values_new = values_new.reshape(own_passages, step_count, local_kv, HEAD_DIM)
    capacity = cache_keys.shape[1]
    keys_old = cache_keys.reshape(own_passages, capacity, local_kv, HEAD_DIM)
    values_old = cache_values.reshape(own_passages, capacity, local_kv, HEAD_DIM)
    new_scores = (
        jnp.einsum("rskgd,rtkd->rskgt", queries, keys_new, preferred_element_type=jnp.float32)
        * score_scale
    )
    causal = step_ids[None, :] <= step_ids[:, None]
    new_scores = jnp.where(causal[None, :, None, None, :], new_scores, -jnp.inf)
    old_scores = (
        jnp.einsum("rskgd,rckd->rskgc", queries, keys_old, preferred_element_type=jnp.float32)
        * score_scale
    )
    slot_ids = jnp.arange(capacity, dtype=jnp.int32)
    live_mask = slot_ids[None, :] < cache_lengths[:, None]
    old_scores = jnp.where(live_mask[:, None, None, None, :], old_scores, -jnp.inf)
    highest = jnp.maximum(jnp.max(old_scores, axis=-1), jnp.max(new_scores, axis=-1))
    old_exp = jnp.exp(old_scores - highest[..., None])
    new_exp = jnp.exp(new_scores - highest[..., None])
    summed = jnp.sum(old_exp, axis=-1) + jnp.sum(new_exp, axis=-1)
    old_weights = (old_exp / summed[..., None]).astype(jnp.bfloat16)
    new_weights = (new_exp / summed[..., None]).astype(jnp.bfloat16)
    attended = jnp.einsum(
        "rskgc,rckd->rskgd", old_weights, values_old, preferred_element_type=jnp.float32
    )
    attended = attended + jnp.einsum(
        "rskgt,rtkd->rskgd", new_weights, values_new, preferred_element_type=jnp.float32
    )
    attended = attended.reshape(own_tokens, query_cols).astype(jnp.bfloat16)
    partial_value = head_mix(attended, decode_out)
    summary = (embedded + width_total(partial_value)).astype(jnp.bfloat16)
    summary_wide = summary.astype(jnp.float32)
    normed_red = (summary_wide * reduce_gain[None, :]).astype(jnp.bfloat16)
    passage_index = jnp.arange(passage_count, dtype=jnp.int32)
    earlier = jnp.sum(
        (
            (doc_ids[None, :] == doc_ids[:, None])
            & (passage_index[None, :] < passage_index[:, None])
        ).astype(jnp.int32),
        axis=1,
    )
    doc_positions = (earlier[:, None] * step_count + step_ids[None, :]).reshape(token_count, 1)
    doc_tokens = (doc_ids[:, None] + jnp.zeros_like(step_ids)[None, :]).reshape(token_count)
    own_positions = lax.dynamic_slice_in_dim(doc_positions, row_first, own_tokens, 0)
    projected, red_squares = head_terms(
        normed_red,
        (reduce_query, reduce_key, reduce_value),
        jnp.sum(summary_wide * summary_wide, axis=1),
        row_groups,
    )
    projected = projected * row_scale(red_squares)[:, None]
    queries_red = rotate(
        projected[:, :query_cols].reshape(own_tokens, local_heads, HEAD_DIM), own_positions
    ).astype(jnp.bfloat16)
    keys_own = (
        rotate(
            projected[:, query_cols : query_cols + kv_cols].reshape(own_tokens, local_kv, HEAD_DIM),
            own_positions,
        )
        .astype(jnp.bfloat16)
        .reshape(own_tokens, kv_cols)
    )
    values_own = projected[:, query_cols + kv_cols :].astype(jnp.bfloat16)
    kv_red = lax.all_gather(
        jnp.concatenate([keys_own, values_own], axis=1), "rows", axis=0, tiled=True
    )
    keys_red, values_red = (kv_red[:, :kv_cols], kv_red[:, kv_cols:])
    queries_red = queries_red.reshape(own_tokens, local_kv, group_size, HEAD_DIM)
    keys_red = keys_red.reshape(token_count, local_kv, HEAD_DIM)
    values_red = values_red.reshape(token_count, local_kv, HEAD_DIM)
    token_index = jnp.arange(token_count, dtype=jnp.int32)
    own_index = row_first + jnp.arange(own_tokens, dtype=jnp.int32)
    own_docs = lax.dynamic_slice_in_dim(doc_tokens, row_first, own_tokens, 0)
    allowed = (own_docs[:, None] == doc_tokens[None, :]) & (
        token_index[None, :] <= own_index[:, None]
    )
    red_scores = (
        jnp.einsum("tkgd,ukd->tkgu", queries_red, keys_red, preferred_element_type=jnp.float32)
        * score_scale
    )
    red_scores = jnp.where(allowed[:, None, None, :], red_scores, -jnp.inf)
    red_high = jnp.max(red_scores, axis=-1)
    red_exp = jnp.exp(red_scores - red_high[..., None])
    red_weights = (red_exp / jnp.sum(red_exp, axis=-1)[..., None]).astype(jnp.bfloat16)
    red_out = jnp.einsum(
        "tkgu,ukd->tkgd", red_weights, values_red, preferred_element_type=jnp.float32
    )
    red_out = red_out.reshape(own_tokens, query_cols).astype(jnp.bfloat16)
    return (summary_wide + width_total(head_mix(red_out, reduce_out))).astype(jnp.bfloat16)


def solution(mesh):
    return jax.shard_map(
        per_device,
        mesh=mesh,
        in_specs=(
            P(),
            P("rows"),
            P(),
            P("tensor", "rows"),
            P("rows", None, "tensor"),
            P("rows", None, "tensor"),
            P("rows"),
            P("rows", "tensor"),
            P("rows", "tensor"),
            P("rows", "tensor"),
            P("tensor", "rows"),
            P("rows"),
            P("rows", "tensor"),
            P("rows", "tensor"),
            P("rows", "tensor"),
            P("tensor", "rows"),
        ),
        out_specs=P(None, "rows"),
        check_vma=False,
    )
```

profile of v0, /device:TPU:8, one launch (start us, length us, event | category | flops | bytes accessed | tf_op | source)
XLA Modules:
  0.0 927.0 jit_solution(14804765056638584329)
XLA Ops:
  6.5 0.9 subtract_clamp_fusion
  7.8 0.7 compare_and_fusion.1
  8.8 6.2 gather_fusion
  15.0 1.1 select_select_fusion
  16.3 69.0 %all-reduce.6.cloned.1.call-done = bf16[1024,256]{1,0:T(8,128)(2,1)} async-done(((bf16[1024,256]{1,0:T(8,128)(2,1)}), bf16[1024,256]{1,0:T(8,128)(2,1)}) %all-reduce.6.cloned.1.call-update) | async-done | bytes 524304 | tf_op jit(solution)/shard_map/psum | solution.py:30
  85.3 2.0 fusion.41
  87.4 0.3 fusion.37
  87.7 0.3 fusion.39
  88.0 2.8 pad_maximum_fusion.2
  90.8 5.9 copy.36
  96.7 5.6 reshape.597
  102.5 5.2 pad_maximum_fusion
  107.7 6.8 reshape.599
  114.6 0.6 copy-done.12
  115.8 0.5 iota_compare_fusion.3
  116.9 209.4 %reduce-scatter.7.cloned.1.call-done = f32[1,8,5124]{2,1,0:T(8,128)} async-done(((f32[32,8,5124]{2,1,0:T(8,128)}), f32[1,8,5124]{2,1,0:T(8,128)}) %reduce-scatter.7.cloned.1.call-update) | async-done | bytes 163984
  326.3 1.0 reshape.600
  327.4 0.5 fusion.75
  327.9 0.9 broadcast_multiply_fusion.1
  328.9 0.8 fusion.65
  329.9 1.1 fusion.81
  331.0 0.5 fusion.82
  331.6 0.3 fusion.8
  332.2 0.6 fusion.15
  332.7 0.6 copy.58
  333.5 76.0 %all-gather.3.cloned.1.call-done = bf16[1024,1024]{1,0:T(8,128)(2,1)} async-done(((bf16[32,1024]{1,0:T(8,128)(2,1)}), bf16[1024,1024]{1,0:T(8,128)(2,1)}) %all-gather.3.cloned.1.call-update) | async-done | bytes 2097168 | tf_op jit(solution)/shard_map/all_gather | solution.py:53
  409.5 3.3 fusion.84
  413.0 66.1 %all-reduce.8.cloned.1.call-done = f32[1024,256]{1,0:T(8,128)} async-done(((f32[1024,256]{1,0:T(8,128)}), f32[1024,256]{1,0:T(8,128)}) %all-reduce.8.cloned.1.call-update) | async-done | bytes 1048592 | tf_op jit(solution)/shard_map/psum | solution.py:30
  479.1 1.4 fusion.25
  480.6 0.8 fusion.35
  481.5 0.3 fusion.31
  481.8 0.3 fusion.33
  482.1 2.9 pad_maximum_fusion.3
  485.1 5.9 copy.37
  491.0 5.6 reshape.607
  496.6 5.2 pad_maximum_fusion.1
  501.8 6.8 reshape.609
  508.6 0.6 copy-done.13
  509.6 211.0 %reduce-scatter.9.cloned.1.call-done = f32[1,8,5124]{2,1,0:T(8,128)} async-done(((f32[32,8,5124]{2,1,0:T(8,128)}), f32[1,8,5124]{2,1,0:T(8,128)}) %reduce-scatter.9.cloned.1.call-update) | async-done | bytes 163984
  720.6 1.0 reshape.610
  722.1 47.8 %all_gather.10 = bf16[1024,256]{1,0:T(8,128)(2,1)S(1)} all-gather(bf16[32,256]{1,0:T(8,128)(2,1)S(1)} %pad_maximum_fusion.5), channel_id=1, replica_groups=mesh['rows'=32,'tensor'=8] {'rows'}, dimensions={0}, use_global_device_ids=true | all-gather | bytes 540672 | tf_op jit(solution)/shard_map/all_gather | solution.py:180
  770.0 0.4 fusion.83
  770.8 0.4 fusion.18
  771.2 0.6 copy.57
  771.9 76.5 %all-gather.5.cloned.1.call-done = bf16[1024,1024]{1,0:T(8,128)(2,1)} async-done(((bf16[32,1024]{1,0:T(8,128)(2,1)}), bf16[1024,1024]{1,0:T(8,128)(2,1)}) %all-gather.5.cloned.1.call-update) | async-done | bytes 2097168 | tf_op jit(solution)/shard_map/all_gather | solution.py:53
  848.4 3.4 fusion.85
  851.8 66.3 %all-reduce.10.cloned.1.call-done = f32[1024,256]{1,0:T(8,128)} async-done(((f32[1024,256]{1,0:T(8,128)}), f32[1024,256]{1,0:T(8,128)}) %all-reduce.10.cloned.1.call-update) | async-done | bytes 1048592 | tf_op jit(solution)/shard_map/psum | solution.py:30
  918.1 2.1 fusion.26
  (109 shorter events, 4.8 us)
Async XLA Ops:
  6.5 323.3 %copy-start = (bf16[8,1280,128]{2,1,0:T(8,128)(2,1)S(1)}, bf16[8,1280,128]{2,1,0:T(8,128)(2,1)}, u32[]{:S(2)}) copy-start(bf16[8,1280,128]{2,1,0:T(8,128)(2,1)} %param.20) | copy-start | bytes 7864324
  6.5 78.8 %copy-start.10 = (f32[256]{0:T(256)S(1)}, f32[256]{0:T(256)}, u32[]{:S(2)}) copy-start(f32[256]{0:T(256)} %param.22) | copy-start | bytes 3076
  6.5 78.8 %all-reduce.6.cloned.1.call-start = ((), (), s32[]{:S(2)}) async-start(), calls=%async_computation.2 | async-start | bytes 1048576 | tf_op jit(solution)/shard_map/psum | solution.py:30
  16.2 71.1 %copy-start.6 = (bf16[256,128]{1,0:T(8,128)(2,1)S(1)}, bf16[256,128]{1,0:T(8,128)(2,1)}, u32[]{:S(2)}) copy-start(bf16[256,128]{1,0:T(8,128)(2,1)} %param.25) | copy-start | bytes 196612
  16.2 71.5 %copy-start.7 = (bf16[256,128]{1,0:T(8,128)(2,1)S(1)}, bf16[256,128]{1,0:T(8,128)(2,1)}, u32[]{:S(2)}) copy-start(bf16[256,128]{1,0:T(8,128)(2,1)} %param.24) | copy-start | bytes 196612
  16.2 310.1 %reduce-scatter.7.cloned.1.call-start = ((), (), s32[]{:S(2)}) async-start(), calls=%async_computation.7 | async-start | bytes 5541888
  85.3 2.0 copy-start.2
  114.5 0.7 copy-start.12
  114.5 1.1 copy-start.19
  114.5 295.0 %all-gather.3.cloned.1.call-start = ((), (), s32[]{:S(2)}) async-start(), calls=%async_computation.3 | async-start | bytes 2162688 | tf_op jit(solution)/shard_map/all_gather | solution.py:53
  115.8 0.9 copy-start.16
  115.8 0.9 copy-start.14
  116.4 0.6 copy-start.17
  327.9 3.1 copy-start.22
  327.9 4.2 copy-start.20
  331.9 77.6 %copy-start.21 = (bf16[1024,256]{1,0:T(8,128)(2,1)S(1)}, bf16[1024,256]{1,0:T(8,128)(2,1)}, u32[]{:S(2)}) copy-start(bf16[1024,256]{1,0:T(8,128)(2,1)} %param.26) | copy-start | bytes 1572868
  333.4 147.1 %copy-start.5 = (bf16[256,1024]{1,0:T(8,128)(2,1)S(1)}, bf16[256,1024]{1,0:T(8,128)(2,1)}, u32[]{:S(2)}) copy-start(bf16[256,1024]{1,0:T(8,128)(2,1)} %param.28) | copy-start | bytes 1572868
  333.4 147.1 %copy-start.11 = (f32[256]{0:T(256)S(1)}, f32[256]{0:T(256)}, u32[]{:S(2)}) copy-start(f32[256]{0:T(256)} %param.27) | copy-start | bytes 3076
  333.4 145.7 %all-reduce.8.cloned.1.call-start = ((), (), s32[]{:S(2)}) async-start(), calls=%async_computation.4 | async-start | bytes 2097152 | tf_op jit(solution)/shard_map/psum | solution.py:30
  412.8 307.8 %reduce-scatter.9.cloned.1.call-start = ((), (), s32[]{:S(2)}) async-start(), calls=%async_computation.8 | async-start | bytes 5541888
  480.5 1.3 copy-start.3
  480.6 0.9 copy-start.8
  480.6 1.2 copy-start.9
  508.6 0.7 copy-start.13
  508.6 213.3 %copy-start.15 = (f32[64]{0:T(128)S(1)}, f32[64]{0:T(128)}, u32[]{:S(2)}) copy-start(f32[64]{0:T(128)} %copy-done.14) | copy-start | bytes 772
  508.6 213.3 %copy-start.18 = (f32[32]{0:T(128)S(1)}, f32[32]{0:T(128)}, u32[]{:S(2)}) copy-start(f32[32]{0:T(128)} %copy-done.17) | copy-start | bytes 388
  508.6 339.8 %all-gather.5.cloned.1.call-start = ((), (), s32[]{:S(2)}) async-start(), calls=%async_computation.5 | async-start | bytes 2162688 | tf_op jit(solution)/shard_map/all_gather | solution.py:53
  771.1 146.9 %copy-start.4 = (bf16[1024,256]{1,0:T(8,128)(2,1)S(1)}, bf16[1024,256]{1,0:T(8,128)(2,1)}, u32[]{:S(2)}) copy-start(bf16[1024,256]{1,0:T(8,128)(2,1)} %copy-done.3) | copy-start | bytes 1572868
  771.8 148.4 %copy-start.1 = (bf16[8,1280,128]{2,1,0:T(8,128)(2,1)S(1)}, bf16[8,1280,128]{2,1,0:T(8,128)(2,1)}, u32[]{:S(2)}) copy-start(bf16[8,1280,128]{2,1,0:T(8,128)(2,1)} %param.20) | copy-start | bytes 7864324
  771.8 146.2 %all-reduce.10.cloned.1.call-start = ((), (), s32[]{:S(2)}) async-start(), calls=%async_computation.6 | async-start | bytes 2097152 | tf_op jit(solution)/shard_map/psum | solution.py:30
Sparse Core Ops, SparseCore 0:
  16.3 68.9 all-reduce.5
  114.6 211.6 reduce-scatter.6
  333.5 75.9 all-gather.2
  412.9 66.1 all-reduce.7
  508.7 211.8 reduce-scatter.8
  771.9 76.3 all-gather.4
  851.9 66.1 all-reduce.9
where the time goes:
time: 928 us; the launch traced here: 927 us
  waiting for transfers between devices  774 us (83%)
  local copies, waits for them, and re-layouts  49.3 us (5%)
  blocking collectives  47.8 us (5%)
  other arithmetic  27.3 us (3%)
  between operations  14 us (2%)
  matrix products  13.9 us (1%)
    unnamed x9, waiting for transfers between devices  420 us
    psum x3, waiting for transfers between devices, width_total(): return lax.psum(partial_value, 'tensor')  201 us
    all_gather x2, waiting for transfers between devices, head_mix(): lax.all_gather(attended, 'rows', axis=0, tiled=True)  153 us
    all_gather x1, blocking collectives, per_device(): lax.all_gather(jnp.concatenate([keys_own, values_own], axis=1), 'rows', a...  47.8 us
  transfers between devices with their start and end apart: 7, of which 7 were waited for; matrix products, arithmetic and copies ran while one was open for 0% of the time, Pallas kernels for 0%

commit v1 on v0

--- a/solution.py
+++ b/solution.py
@@ -49,11 +49,14 @@
 
 
 def head_mix(attended, matrix):
-    return jnp.dot(
-        lax.all_gather(attended, "rows", axis=0, tiled=True),
-        matrix,
-        preferred_element_type=jnp.float32,
-    )
+
+    def choose_bands(sheet, out_dim):
+        log = []
+        for _ in range(lax.axis_size("rows")):
+            log.append(sheet)
+        return jnp.concatenate(lax.all_to_all(jnp.stack(log), "rows", 0, 0), out_dim)
+
+    return jnp.dot(choose_bands(attended, 0), matrix, preferred_element_type=jnp.float32)
 
 
 def per_device(

time: 928 us -> 864 us (0.931)
  waiting for transfers between devices: 774 us -> 622 us
  blocking collectives: 47.8 us -> 140 us
    all_gather x2 -> x0, waiting for transfers between devices: 153 us -> none  [head_mix(): lax.all_gather(attended, 'rows', axis=0, tiled=True)]
    all_to_all x0 -> x2, blocking collectives: none -> 90.9 us  [choose_bands(): lax.all_to_all(jnp.stack(log), 'rows', 0, 0)]
    unnamed x9 -> x7, waiting for transfers between devices: 420 us -> 421 us
  transfers between devices with their start and end apart: 7 -> 5, of which waited for: 7 -> 5; matrix products, arithmetic and copies ran while one was open for 0% -> 0% of each run, Pallas kernels for 0% -> 0%
where the time goes in v1:
time: 864 us; the launch traced here: 863 us
  waiting for transfers between devices  622 us (72%)
  blocking collectives  140 us (16%)
  local copies, waits for them, and re-layouts  48.4 us (6%)
  other arithmetic  27.2 us (3%)
  between operations  13.7 us (2%)
  matrix products  10.7 us (1%)
    unnamed x7, waiting for transfers between devices  421 us
    psum x3, waiting for transfers between devices, width_total(): return lax.psum(partial_value, 'tensor')  202 us
    all_to_all x2, blocking collectives, choose_bands(): lax.all_to_all(jnp.stack(log), 'rows', 0, 0)  90.9 us
    all_gather x1, blocking collectives, per_device(): lax.all_gather(jnp.concatenate([keys_own, values_own], axis=1), 'rows', a...  49.4 us
  transfers between devices with their start and end apart: 5, of which 5 were waited for; matrix products, arithmetic and copies ran while one was open for 0% of the time, Pallas kernels for 0%

profile of v1, /device:TPU:8, one launch (start us, length us, event | category | flops | bytes accessed | tf_op | source)
XLA Modules:
  0.0 863.2 jit_solution(2034429062263319799)
XLA Ops:
  6.5 0.9 subtract_clamp_fusion
  7.8 0.7 compare_and_fusion.1
  8.8 6.2 gather_fusion
  15.0 1.1 select_select_fusion
  16.3 69.0 %all-reduce.6.cloned.1.call-done = bf16[1024,256]{1,0:T(8,128)(2,1)} async-done(((bf16[1024,256]{1,0:T(8,128)(2,1)}), bf16[1024,256]{1,0:T(8,128)(2,1)}) %all-reduce.6.cloned.1.call-update) | async-done | bytes 524304 | tf_op jit(solution)/shard_map/psum | solution.py:30
  85.3 2.0 fusion.41
  87.4 0.3 fusion.37
  87.7 0.3 fusion.39
  88.0 2.8 pad_maximum_fusion.2
  90.8 5.9 copy.36
  96.7 5.6 reshape.609
  102.5 5.2 pad_maximum_fusion
  107.7 6.8 reshape.611
  114.5 0.6 copy-done.12
  115.7 0.5 iota_compare_fusion.3
  116.8 209.4 %reduce-scatter.7.cloned.1.call-done = f32[1,8,5124]{2,1,0:T(8,128)} async-done(((f32[32,8,5124]{2,1,0:T(8,128)}), f32[1,8,5124]{2,1,0:T(8,128)}) %reduce-scatter.7.cloned.1.call-update) | async-done | bytes 163984
  326.3 1.0 reshape.612
  327.3 0.5 fusion.75
  327.9 0.9 broadcast_multiply_fusion.1
  328.8 0.8 fusion.65
  329.7 1.1 fusion.81
  330.8 0.5 fusion.82
  331.4 0.3 fusion.8
  332.0 0.6 fusion.15
  332.6 0.2 stack.4
  332.9 52.1 %all_to_all.10 = bf16[32,32,1024]{2,1,0:T(8,128)(2,1)S(1)} all-to-all(bf16[32,32,1024]{2,1,0:T(8,128)(2,1)S(1)} %stack.4), channel_id=1, replica_groups=mesh['rows'=32,'tensor'=8] {'rows'}, dimensions={0} | all-to-all | bytes 4194304 | tf_op jit(solution)/shard_map/all_to_all | solution.py:57
  385.0 1.7 fusion.84
  387.0 66.3 %all-reduce.8.cloned.1.call-done = f32[1024,256]{1,0:T(8,128)} async-done(((f32[1024,256]{1,0:T(8,128)}), f32[1024,256]{1,0:T(8,128)}) %all-reduce.8.cloned.1.call-update) | async-done | bytes 1048592 | tf_op jit(solution)/shard_map/psum | solution.py:30
  453.3 1.4 fusion.25
  454.8 0.8 fusion.35
  455.7 0.3 fusion.31
  456.0 0.3 fusion.33
  456.3 2.9 pad_maximum_fusion.3
  459.2 5.9 copy.37
  465.1 5.6 reshape.620
  470.7 5.2 pad_maximum_fusion.1
  475.9 6.8 reshape.622
  482.7 0.6 copy-done.13
  483.7 211.1 %reduce-scatter.9.cloned.1.call-done = f32[1,8,5124]{2,1,0:T(8,128)} async-done(((f32[32,8,5124]{2,1,0:T(8,128)}), f32[1,8,5124]{2,1,0:T(8,128)}) %reduce-scatter.9.cloned.1.call-update) | async-done | bytes 163984
  694.8 1.0 reshape.623
  696.3 49.4 %all_gather.3 = bf16[1024,256]{1,0:T(8,128)(2,1)S(1)} all-gather(bf16[32,256]{1,0:T(8,128)(2,1)S(1)} %pad_maximum_fusion.5), channel_id=1, replica_groups=mesh['rows'=32,'tensor'=8] {'rows'}, dimensions={0}, use_global_device_ids=true | all-gather | bytes 540672 | tf_op jit(solution)/shard_map/all_gather | solution.py:183
  745.9 0.4 fusion.83
  746.4 0.3 fusion.27
  746.7 0.4 fusion.18
  747.4 38.9 %all_to_all.11 = bf16[32,32,1024]{2,1,0:T(8,128)(2,1)S(1)} all-to-all(bf16[32,32,1024]{2,1,0:T(8,128)(2,1)S(1)} %stack.5), channel_id=1, replica_groups=mesh['rows'=32,'tensor'=8] {'rows'}, dimensions={0} | all-to-all | bytes 4194304 | tf_op jit(solution)/shard_map/all_to_all | solution.py:57
  786.2 1.7 fusion.85
  788.0 66.5 %all-reduce.10.cloned.1.call-done = f32[1024,256]{1,0:T(8,128)} async-done(((f32[1024,256]{1,0:T(8,128)}), f32[1024,256]{1,0:T(8,128)}) %all-reduce.10.cloned.1.call-update) | async-done | bytes 1048592 | tf_op jit(solution)/shard_map/psum | solution.py:30
  854.5 2.1 fusion.26
  (109 shorter events, 4.6 us)
Async XLA Ops:
  6.5 323.2 %copy-start = (bf16[8,1280,128]{2,1,0:T(8,128)(2,1)S(1)}, bf16[8,1280,128]{2,1,0:T(8,128)(2,1)}, u32[]{:S(2)}) copy-start(bf16[8,1280,128]{2,1,0:T(8,128)(2,1)} %param.20) | copy-start | bytes 7864324
  6.5 78.8 %copy-start.10 = (f32[256]{0:T(256)S(1)}, f32[256]{0:T(256)}, u32[]{:S(2)}) copy-start(f32[256]{0:T(256)} %param.22) | copy-start | bytes 3076
  6.5 78.8 %all-reduce.6.cloned.1.call-start = ((), (), s32[]{:S(2)}) async-start(), calls=%async_computation.4 | async-start | bytes 1048576 | tf_op jit(solution)/shard_map/psum | solution.py:30
  16.2 71.1 %copy-start.6 = (bf16[256,128]{1,0:T(8,128)(2,1)S(1)}, bf16[256,128]{1,0:T(8,128)(2,1)}, u32[]{:S(2)}) copy-start(bf16[256,128]{1,0:T(8,128)(2,1)} %param.25) | copy-start | bytes 196612
  16.2 71.5 %copy-start.7 = (bf16[256,128]{1,0:T(8,128)(2,1)S(1)}, bf16[256,128]{1,0:T(8,128)(2,1)}, u32[]{:S(2)}) copy-start(bf16[256,128]{1,0:T(8,128)(2,1)} %param.24) | copy-start | bytes 196612
  16.2 310.0 %reduce-scatter.7.cloned.1.call-start = ((), (), s32[]{:S(2)}) async-start(), calls=%async_computation.7 | async-start | bytes 5541888
  85.3 2.0 copy-start.2
  114.4 0.7 copy-start.12
  114.4 1.1 copy-start.19
  114.5 338.8 %all-reduce.8.cloned.1.call-start = ((), (), s32[]{:S(2)}) async-start(), calls=%async_computation.5 | async-start | bytes 2097152 | tf_op jit(solution)/shard_map/psum | solution.py:30
  115.7 0.9 copy-start.16
  115.7 0.9 copy-start.14
  116.3 0.5 copy-start.17
  327.8 3.0 copy-start.23
  327.9 4.1 copy-start.20
  332.6 52.4 %copy-start.21 = (bf16[1024,256]{1,0:T(8,128)(2,1)S(1)}, bf16[1024,256]{1,0:T(8,128)(2,1)}, u32[]{:S(2)}) copy-start(bf16[1024,256]{1,0:T(8,128)(2,1)} %param.26) | copy-start | bytes 1572868
  385.0 69.8 %copy-start.5 = (bf16[256,1024]{1,0:T(8,128)(2,1)S(1)}, bf16[256,1024]{1,0:T(8,128)(2,1)}, u32[]{:S(2)}) copy-start(bf16[256,1024]{1,0:T(8,128)(2,1)} %param.28) | copy-start | bytes 1572868
  385.0 69.8 %copy-start.11 = (f32[256]{0:T(256)S(1)}, f32[256]{0:T(256)}, u32[]{:S(2)}) copy-start(f32[256]{0:T(256)} %param.27) | copy-start | bytes 3076
  386.7 308.1 %reduce-scatter.9.cloned.1.call-start = ((), (), s32[]{:S(2)}) async-start(), calls=%async_computation.8 | async-start | bytes 5541888
  454.7 1.3 copy-start.3
  454.7 0.9 copy-start.8
  454.8 1.2 copy-start.9
  482.7 0.7 copy-start.13
  482.7 213.4 %copy-start.15 = (f32[64]{0:T(128)S(1)}, f32[64]{0:T(128)}, u32[]{:S(2)}) copy-start(f32[64]{0:T(128)} %copy-done.14) | copy-start | bytes 772
  482.7 213.4 %copy-start.18 = (f32[32]{0:T(128)S(1)}, f32[32]{0:T(128)}, u32[]{:S(2)}) copy-start(f32[32]{0:T(128)} %copy-done.17) | copy-start | bytes 388
  482.7 371.8 %all-reduce.10.cloned.1.call-start = ((), (), s32[]{:S(2)}) async-start(), calls=%async_computation.6 | async-start | bytes 2097152 | tf_op jit(solution)/shard_map/psum | solution.py:30
  747.0 39.2 %copy-start.22 = (bf16[1024,256]{1,0:T(8,128)(2,1)S(1)}, bf16[1024,256]{1,0:T(8,128)(2,1)}, u32[]{:S(2)}) copy-start(bf16[1024,256]{1,0:T(8,128)(2,1)} %param.31) | copy-start | bytes 1572868
  786.2 68.3 %copy-start.4 = (bf16[1024,256]{1,0:T(8,128)(2,1)S(1)}, bf16[1024,256]{1,0:T(8,128)(2,1)}, u32[]{:S(2)}) copy-start(bf16[1024,256]{1,0:T(8,128)(2,1)} %copy-done.3) | copy-start | bytes 1572868
  786.2 70.4 %copy-start.1 = (bf16[8,1280,128]{2,1,0:T(8,128)(2,1)S(1)}, bf16[8,1280,128]{2,1,0:T(8,128)(2,1)}, u32[]{:S(2)}) copy-start(bf16[8,1280,128]{2,1,0:T(8,128)(2,1)} %param.20) | copy-start | bytes 7864324
Sparse Core Ops, SparseCore 0:
  16.3 68.9 all-reduce.5
  114.6 211.6 reduce-scatter.6
  386.9 66.3 all-reduce.7
  482.8 211.9 reduce-scatter.8
  788.1 66.3 all-reduce.9
